TPU v7x, 256 devices: a whole 4x4x8 slice. The times are simulated.
256 devices in a mesh: seq: 32 (over x_hi, z, core), ch: 8 (over y, x_lo).
Axes of the slice: x: 4 (x_hi: 2, x_lo: 2; x = x_hi * 2 + x_lo), y: 4, z: 8, core: 2. Of those that a mesh axis runs over, the one named last changes fastest.
Arguments:
- hidden: bfloat16 [4096, 2048], P('seq', 'ch'), may hold values from -400 to 400, as said below
- tokens: int32 [4096], replicated, may hold values from 0 to 3
- edit_bounds: int32 [8, 2], replicated, may hold values from 0 to 4095
- norm_gain: float32 [2048], replicated, may hold values from 0.1 to 1.9
- base_embed: float32 [4, 2048], replicated, may hold values from -6 to 6
- w_in: bfloat16 [2, 2048, 4096], P(None, None, 'ch'), may hold values from -0.125 to 0.125
- conv_w: float32 [4, 4096], P(None, 'ch'), may hold values from -3 to 3
- conv_b: float32 [4096], P('ch'), may hold values from -3 to 3
- proj_bc: bfloat16 [32, 4096], P(None, 'ch'), may hold values from -0.1875 to 0.1875
- decay_rate: float32 [16, 4096], P(None, 'ch'), may hold values from 9.765625e-06 to 0.11, as said below
- skip_gain: float32 [4096], P('ch'), may hold values from -4 to 4
- w_out: bfloat16 [4096, 2048], P('ch'), may hold values from -0.09375 to 0.09375
Outputs:
- mixed: bfloat16 [4096, 2048], P('seq', 'ch')
Inputs may be any that keep to these rules, and one draw needn't show every extreme that they name: The hidden states have row and column scales that differ. `decay_rate`: each entry is a positive decay rate per position. `edit_bounds`: positions in the window; a span's start and end come in no fixed order and may coincide with others.
All inputs are finite; a program needn't handle non-finite values.
Results may differ from a plain program's by a relative error of at most 0.014.
Values may be sent and summed in bfloat16 or wider, within the bound.
A program may use at most 64 MiB of HBM per device.

v0:
```python
import jax
import jax.numpy as jnp
from jax import lax
from jax.sharding import PartitionSpec as P

CONV = 4


epsilon = 1e-05


def from_partner(block, axis, apart):
    count = lax.axis_size(axis)
    route = []
    for low in range(count):
        high = low | 1 << apart
        if high != low and high < count:
            route += [(low, high), (high, low)]
    return lax.ppermute(block, axis, route)


def passed_along(block, axis, distance):
    devices = range(lax.axis_size(axis))
    route = [(i - distance, i) for i in devices if i - distance in devices]
    return lax.ppermute(block, axis, route)


def carried_in(part, axis, combine, identity):
    place = lax.axis_index(axis)
    gathered = jax.tree.map(lambda a: lax.all_gather(a, axis), part)
    state = jax.tree.map(lambda a, e: jnp.zeros_like(a) + jnp.asarray(e, a.dtype), part, identity)

    def one(step, state):
        return combine(
            state, jax.tree.map(lambda a: lax.dynamic_index_in_dim(a, step, 0, False), gathered)
        )

    return lax.fori_loop(0, place, one, state)


def link(before, follow):
    return (before[0] * follow[0], before[1] * follow[0] + follow[1])


def link_pair(before, follow):
    return link(before[0:2], follow[0:2]) + link(before[2:4], follow[2:4])


def keep_rows(places, edit_bounds):
    hit_count = jnp.sum(
        (places[:, None] == edit_bounds.reshape(-1)[None, :]).astype(jnp.float32), axis=1
    )
    return 1.0 / (1.0 + hit_count)


def norm_rows(rows, bases, norm_gain, base_embed):
    row_values = rows.astype(jnp.float32)
    inv_rms = lax.rsqrt(jnp.mean(row_values * row_values, axis=1, keepdims=True) + epsilon)
    one_hot = (bases[:, None] == jnp.arange(4, dtype=jnp.int32)[None, :]).astype(jnp.float32)
    embedded = one_hot[:, 0:1] * base_embed[0][None, :]
    for base_index in range(1, 4):
        embedded = (
            embedded + one_hot[:, base_index : base_index + 1] * base_embed[base_index][None, :]
        )
    return (row_values * inv_rms * norm_gain[None, :] + embedded).astype(jnp.bfloat16)


def run_chain(
    start_state, keep_both, inputs_b, inputs_r, mixed_both, decay_mult, drive_gain, want_rows
):
    row_count = mixed_both.shape[1]
    inner_width = mixed_both.shape[2]
    state_size = inputs_b.shape[1]
    turns = 8
    per_turn = row_count // turns
    keep_blocks = keep_both.T.reshape(turns, per_turn, 2)
    b_blocks = inputs_b.transpose(2, 0, 1).reshape(turns, per_turn, 2, state_size)
    r_blocks = inputs_r.transpose(2, 0, 1).reshape(turns, per_turn, 2, state_size)
    x_blocks = mixed_both.transpose(1, 0, 2).reshape(turns, per_turn, 2, inner_width)

    def turn_step(state, block):
        keep_block, b_block, r_block, x_block = block
        outputs = []
        for row_index in range(per_turn):
            x_float = x_block[row_index].astype(jnp.float32)
            state = (
                keep_block[row_index][:, None, None] * decay_mult[None] * state
                + drive_gain[None] * b_block[row_index][:, :, None] * x_float[:, None, :]
            )
            if want_rows:
                outputs.append(jnp.sum(r_block[row_index][:, :, None] * state, axis=1))
        if want_rows:
            return (state, jnp.stack(outputs))
        return (state, jnp.zeros((), jnp.float32))

    final_state, produced = lax.scan(
        turn_step, start_state, (keep_blocks, b_blocks, r_blocks, x_blocks)
    )
    if want_rows:
        return (final_state, produced.reshape(row_count, 2, inner_width).transpose(1, 0, 2))
    return (final_state, None)


def body(
    hidden,
    tokens,
    edit_bounds,
    norm_gain,
    base_embed,
    w_in,
    conv_w,
    conv_b,
    proj_bc,
    decay_rate,
    skip_gain,
    w_out,
):
    row_count = hidden.shape[0]
    seq_count = lax.axis_size("seq")
    where_am = lax.axis_index("seq")
    levels = seq_count.bit_length() - 1
    own_bases = lax.dynamic_slice_in_dim(tokens, where_am * row_count, row_count)
    partner_shard = hidden
    for bit_index in range(levels):
        partner_shard = from_partner(partner_shard, "seq", bit_index)
    owner_dev = seq_count - 1 - where_am
    to_gather = jnp.stack([hidden, partner_shard])
    gathered = lax.all_gather(to_gather, "ch", axis=2, tiled=True)
    normed = norm_rows(gathered[0], own_bases, norm_gain, base_embed)
    far_bases = lax.dynamic_slice_in_dim(tokens, owner_dev * row_count, row_count)
    partner = norm_rows(gathered[1], far_bases, norm_gain, base_embed)
    offsets = jnp.arange(row_count, dtype=jnp.int32)
    keep_ahead = keep_rows(where_am * row_count + offsets, edit_bounds)
    back_rows = partner[::-1, ::-1]
    keep_back = keep_rows(owner_dev * row_count + row_count - 1 - offsets, edit_bounds)
    stacked = jnp.concatenate([normed, back_rows], axis=0)
    both_proj = lax.dot_general(
        stacked, w_in, (((1,), (1,)), ((), ())), preferred_element_type=jnp.float32
    ).astype(jnp.bfloat16)
    x_part = both_proj[:, 0, :].reshape(2, row_count, -1)
    z_part = both_proj[:, 1, :].reshape(2, row_count, -1)
    rims = x_part[:, row_count - CONV + 1 :, :]
    rims_in = passed_along(rims, "seq", 1)
    padded = jnp.concatenate([rims_in, x_part], axis=1)
    conv_sum = conv_b[None, None, :] + jnp.zeros(x_part.shape, jnp.float32)
    for tap_index in range(CONV):
        conv_sum = (
            conv_sum
            + padded[:, tap_index : tap_index + row_count, :].astype(jnp.float32)
            * conv_w[tap_index][None, None, :]
        )
    mixed_in = jax.nn.silu(conv_sum).astype(jnp.bfloat16)
    partial_bc = jnp.einsum("kc,slc->skl", proj_bc, mixed_in, preferred_element_type=jnp.float32)
    inputs_bc = lax.psum(partial_bc, "ch")
    state_size = decay_rate.shape[0]
    inputs_b = inputs_bc[:, :state_size]
    inputs_r = inputs_bc[:, state_size:]
    decay_mult = jnp.exp(-decay_rate)
    drive_gain = jnp.sqrt(-jnp.expm1(-2.0 * decay_rate))
    keep_both = jnp.stack([keep_ahead, keep_back])
    zero_state = jnp.zeros((2,) + decay_rate.shape, jnp.float32)
    local_end, unused = run_chain(
        zero_state, keep_both, inputs_b, inputs_r, mixed_in, decay_mult, drive_gain, False
    )
    block_decay = jnp.exp(-float(row_count) * decay_rate)
    pass_ahead = jnp.prod(keep_ahead) * block_decay
    pass_back = jnp.prod(keep_back) * block_decay
    identity_pair = (jnp.ones_like(decay_mult), jnp.zeros_like(decay_mult))
    carried = carried_in(
        (pass_ahead, local_end[0], pass_back, local_end[1]),
        "seq",
        link_pair,
        identity_pair + identity_pair,
    )
    carry_fore = carried[1]
    carry_aft = carried[3]
    entering = jnp.stack([carry_fore, carry_aft])
    final_unused, read_rows = run_chain(
        entering, keep_both, inputs_b, inputs_r, mixed_in, decay_mult, drive_gain, True
    )
    y_out = read_rows + skip_gain[None, None, :] * mixed_in.astype(jnp.float32)
    gated = (y_out * jax.nn.silu(z_part.astype(jnp.float32))).astype(jnp.bfloat16)
    gated_ahead = gated[0]
    gated_back = gated[1]
    for bit_index in range(levels):
        gated_back = from_partner(gated_back, "seq", bit_index)
    aligned = gated_back[::-1]
    summed = (
        jnp.dot(gated_ahead, w_out, preferred_element_type=jnp.float32)
        + jnp.dot(aligned, w_out, preferred_element_type=jnp.float32)[:, ::-1]
    )
    return lax.psum_scatter(summed.astype(jnp.bfloat16), "ch", scatter_dimension=1, tiled=True)


def solution(mesh):
    placed = (
        P("seq", "ch"),
        P(),
        P(),
        P(),
        P(),
        P(None, None, "ch"),
        P(None, "ch"),
        P("ch"),
        P(None, "ch"),
        P(None, "ch"),
        P("ch"),
        P("ch", None),
    )
    return jax.shard_map(
        body, mesh=mesh, in_specs=placed, out_specs=P("seq", "ch"), check_vma=False
    )
```

profile of v0, /device:TPU:1, one launch (start us, length us, event | category | flops | bytes accessed | tf_op | source)
XLA Modules:
  0.0 524.2 jit_solution(1080955099993510452)
XLA Ops:
  6.5 3.2 collective-permute-start
  10.9 3.1 collective-permute-done.1
  15.8 2.9 collective-permute-done.2
  18.7 5.2 collective-permute-start.3
  25.7 2.7 collective-permute-start.4
  33.6 2.6 fusion.187
  39.6 36.2 %all-gather.8.cloned.1.call-done = bf16[2,128,2048]{2,1,0:T(8,128)(2,1)} async-done(((bf16[2,128,256]{2,1,0:T(8,128)(2,1)}), bf16[2,128,2048]{2,1,0:T(8,128)(2,1)}) %all-gather.8.cloned.1.call-update) | async-done | bytes 1048592 | tf_op jit(solution)/shard_map/all_gather | solution.py:128
  77.3 2.9 fusion.171
  82.0 3.6 convolution_convert_fusion
  85.7 8.1 %collective-permute-start.5 = (bf16[2,3,512]{2,1,0:T(4,128)(2,1)S(1)}, bf16[2,3,512]{2,1,0:T(4,128)(2,1)S(1)}, u32[]{:S(2)}, u32[]{:S(2)}) collective-permute-start(bf16[2,3,512]{2,1,0:T(4,128)(2,1)S(1)} %slice.623), channel_id=1, source_target_pairs={{0,8},{8,16},{16,24},{24,32},{32,40},{40,48},{48,56},{56,64},{64,7... | collective-permute-start | bytes 18440 | tf_op jit(solution)/shard_map/ppermute | solution.py:25
  95.4 26.8 %psum.7 = f32[2,32,128]{2,1,0:T(8,128)S(1)} all-reduce(f32[2,32,128]{2,1,0:T(8,128)S(1)} %convolution_bitcast_fusion), channel_id=1, replica_groups=mesh['seq'=32,'ch'=8] {'ch'}, use_global_device_ids=true, to_apply=%region_5.6 | all-reduce | flops 8192 | bytes 65536 | tf_op jit(solution)/shard_map/psum | solution.py:154
  122.3 5.1 while.41
  128.9 33.8 %all-gather.16.cloned.1.call-done = f32[512,512]{1,0:T(8,128)} async-done(((f32[16,512]{1,0:T(8,128)}), f32[512,512]{1,0:T(8,128)}) %all-gather.16.cloned.1.call-update) | async-done | bytes 1048592 | tf_op jit(solution)/shard_map/all_gather | solution.py:30
  162.7 77.5 %all-gather.14.cloned.1.call-done = f32[512,512]{1,0:T(8,128)} async-done(((f32[16,512]{1,0:T(8,128)}), f32[512,512]{1,0:T(8,128)}) %all-gather.14.cloned.1.call-update) | async-done | bytes 1048592 | tf_op jit(solution)/shard_map/all_gather | solution.py:30
  240.2 77.3 %all-gather.10.cloned.1.call-done = f32[32,16,512]{2,1,0:T(8,128)} async-done(((f32[1,16,512]{2,1,0:T(8,128)}), f32[32,16,512]{2,1,0:T(8,128)}) %all-gather.10.cloned.1.call-update) | async-done | bytes 1048592 | tf_op jit(solution)/shard_map/all_gather | solution.py:30
  317.5 77.3 %all-gather.12.cloned.1.call-done = f32[32,16,512]{2,1,0:T(8,128)} async-done(((f32[1,16,512]{2,1,0:T(8,128)}), f32[32,16,512]{2,1,0:T(8,128)}) %all-gather.12.cloned.1.call-update) | async-done | bytes 1048592 | tf_op jit(solution)/shard_map/all_gather | solution.py:30
  395.7 16.8 %while.40 = (s32[]{:T(128)}, f32[2,16,512]{2,1,0:T(8,128)S(1)}, f32[8,16,2,512]{3,2,1,0:T(2,128)}, f32[8,16,2]{2,1,0:T(8,128)S(1)}, f32[16,512]{1,0:T(8,128)S(1)...) while((s32[]{:T(128)}, f32[2,16,512]{2,1,0:T(8,128)S(1)}, ...), condition=%wide.region_28.29_spmd, body=%wide.region_11.28_spmd.sunk | while | flops 2818065 | bytes 1473593 | solution.py:96
  417.3 3.7 collective-permute-done.7
  421.0 5.2 collective-permute-start.8
  426.2 6.0 %collective-permute-done.8 = bf16[128,512]{1,0:T(8,128)(2,1)S(1)} collective-permute-done((bf16[128,512]{1,0:T(8,128)(2,1)S(1)}, bf16[128,512]{1,0:T(8,128)(2,1)S(1)}, u32[]{:S(2)}, u32[]{:S(2)}) %collective-permute-start.8) | collective-permute-done | bytes 131104 | tf_op jit(solution)/shard_map/ppermute | solution.py:19
  432.2 9.6 %collective-permute-start.9 = (bf16[128,512]{1,0:T(8,128)(2,1)S(1)}, bf16[128,512]{1,0:T(8,128)(2,1)S(1)}, u32[]{:S(2)}, u32[]{:S(2)}) collective-permute-start(bf16[128,512]{1,0:T(8,128)(2,1)S(1)} %collective-permute-done.8), channel_id=1, source_target_pairs={{0,64},{64,0},{8,72},{72,8},{16,80},{80,16},{24,88},{88,24},{32,96... | collective-permute-start | bytes 393224 | tf_op jit(solution)/shard_map/ppermute | solution.py:19
  444.2 14.4 %collective-permute-start.10 = (bf16[128,512]{1,0:T(8,128)(2,1)S(1)}, bf16[128,512]{1,0:T(8,128)(2,1)S(1)}, u32[]{:S(2)}, u32[]{:S(2)}) collective-permute-start(bf16[128,512]{1,0:T(8,128)(2,1)S(1)} %collective-permute-done.9), channel_id=1, source_target_pairs={{0,128},{128,0},{8,136},{136,8},{16,144},{144,16},{24,152},{152,24... | collective-permute-start | bytes 393224 | tf_op jit(solution)/shard_map/ppermute | solution.py:19
  462.6 9.3 %rev.11 = f32[128,2048]{1,0:T(8,128)} reverse(f32[128,2048]{1,0:T(8,128)} %fusion.199), dimensions={1} | reverse | bytes 2097152 | tf_op jit(solution)/shard_map/rev | solution.py:190
  474.1 43.3 %reduce-scatter.2.cloned.1.call-done = bf16[128,256]{1,0:T(8,128)(2,1)} async-done(((bf16[128,2048]{1,0:T(8,128)(2,1)}), bf16[128,256]{1,0:T(8,128)(2,1)}) %reduce-scatter.2.cloned.1.call-update) | async-done | bytes 65552 | tf_op jit(solution)/shard_map/reduce_scatter | solution.py:192
  (303 shorter events, 55.4 us)
Async XLA Ops:
  6.5 452.0 %copy-start = (bf16[512,2048]{1,0:T(8,128)(2,1)S(1)}, bf16[512,2048]{1,0:T(8,128)(2,1)}, u32[]{:S(2)}) copy-start(bf16[512,2048]{1,0:T(8,128)(2,1)} %param.29) | copy-start | bytes 6291460
  6.5 69.2 %all-gather.8.cloned.1.call-start = ((), (), s32[]{:S(2)}) async-start(), calls=%async_computation.1 | async-start | bytes 1179648 | tf_op jit(solution)/shard_map/all_gather | solution.py:128
  6.5 4.3 collective-permute-start
  10.9 3.1 collective-permute-start.1
  14.0 4.7 collective-permute-start.2
  18.7 7.0 %collective-permute-start.3 = (bf16[128,256]{1,0:T(8,128)(2,1)S(1)}, bf16[128,256]{1,0:T(8,128)(2,1)S(1)}, u32[]{:S(2)}, u32[]{:S(2)}) collective-permute-start(bf16[128,256]{1,0:T(8,128)(2,1)S(1)} %collective-permute-done.2), channel_id=1, source_target_pairs={{0,64},{64,0},{8,72},{72,8},{16,80},{80,16},{24,88},{88,24},{32,96... | collective-permute-start | bytes 196616 | tf_op jit(solution)/shard_map/ppermute | solution.py:19
  25.7 4.6 collective-permute-start.4
  31.9 130.8 %all-gather.16.cloned.1.call-start = ((), (), s32[]{:S(2)}) async-start(), calls=%async_computation.6 | async-start | bytes 1081344 | tf_op jit(solution)/shard_map/all_gather | solution.py:30
  36.2 204.0 %all-gather.14.cloned.1.call-start = ((), (), s32[]{:S(2)}) async-start(), calls=%async_computation.5 | async-start | bytes 1081344 | tf_op jit(solution)/shard_map/all_gather | solution.py:30
  37.0 280.5 %all-gather.10.cloned.1.call-start = ((), (), s32[]{:S(2)}) async-start(), calls=%async_computation.2 | async-start | bytes 1081344 | tf_op jit(solution)/shard_map/all_gather | solution.py:30
  82.0 12.6 %copy-start.2 = (f32[512]{0:T(512)S(1)}, f32[512]{0:T(512)}, u32[]{:S(2)}) copy-start(f32[512]{0:T(512)} %param.25) | copy-start | bytes 6148
  85.6 9.6 %copy-start.1 = (bf16[32,512]{1,0:T(8,128)(2,1)S(1)}, bf16[32,512]{1,0:T(8,128)(2,1)}, u32[]{:S(2)}) copy-start(bf16[32,512]{1,0:T(8,128)(2,1)} %param.26) | copy-start | bytes 98308
  85.7 8.9 %collective-permute-start.5 = (bf16[2,3,512]{2,1,0:T(4,128)(2,1)S(1)}, bf16[2,3,512]{2,1,0:T(4,128)(2,1)S(1)}, u32[]{:S(2)}, u32[]{:S(2)}) collective-permute-start(bf16[2,3,512]{2,1,0:T(4,128)(2,1)S(1)} %slice.623), channel_id=1, source_target_pairs={{0,8},{8,16},{16,24},{24,32},{32,40},{40,48},{48,56},{56,64},{64,7... | collective-permute-start | bytes 18440 | tf_op jit(solution)/shard_map/ppermute | solution.py:25
  128.1 266.7 %all-gather.12.cloned.1.call-start = ((), (), s32[]{:S(2)}) async-start(), calls=%async_computation.3 | async-start | bytes 1081344 | tf_op jit(solution)/shard_map/all_gather | solution.py:30
  128.7 388.7 %reduce-scatter.2.cloned.1.call-start = ((), (), s32[]{:S(2)}) async-start(), calls=%async_computation.4 | async-start | bytes 589824 | tf_op jit(solution)/shard_map/reduce_scatter | solution.py:192
  395.7 16.8 %copy-start.3 = (f32[512]{0:T(512)S(1)}, f32[512]{0:T(512)}, u32[]{:S(2)}) copy-start(f32[512]{0:T(512)} %param.28) | copy-start | bytes 6148
  413.7 1.4 collective-permute-start.6
  415.2 5.9 %collective-permute-start.7 = (bf16[128,512]{1,0:T(8,128)(2,1)S(1)}, bf16[128,512]{1,0:T(8,128)(2,1)S(1)}, u32[]{:S(2)}, u32[]{:S(2)}) collective-permute-start(bf16[128,512]{1,0:T(8,128)(2,1)S(1)} %collective-permute-done.6), channel_id=1, source_target_pairs={{0,16},{16,0},{8,24},{24,8},{32,48},{48,32},{40,56},{56,40},{64,80... | collective-permute-start | bytes 393224 | tf_op jit(solution)/shard_map/ppermute | solution.py:19
  421.0 11.2 %collective-permute-start.8 = (bf16[128,512]{1,0:T(8,128)(2,1)S(1)}, bf16[128,512]{1,0:T(8,128)(2,1)S(1)}, u32[]{:S(2)}, u32[]{:S(2)}) collective-permute-start(bf16[128,512]{1,0:T(8,128)(2,1)S(1)} %collective-permute-done.7), channel_id=1, source_target_pairs={{0,32},{32,0},{8,40},{40,8},{16,48},{48,16},{24,56},{56,24},{64,96... | collective-permute-start | bytes 393224 | tf_op jit(solution)/shard_map/ppermute | solution.py:19
  432.2 12.0 %collective-permute-start.9 = (bf16[128,512]{1,0:T(8,128)(2,1)S(1)}, bf16[128,512]{1,0:T(8,128)(2,1)S(1)}, u32[]{:S(2)}, u32[]{:S(2)}) collective-permute-start(bf16[128,512]{1,0:T(8,128)(2,1)S(1)} %collective-permute-done.8), channel_id=1, source_target_pairs={{0,64},{64,0},{8,72},{72,8},{16,80},{80,16},{24,88},{88,24},{32,96... | collective-permute-start | bytes 393224 | tf_op jit(solution)/shard_map/ppermute | solution.py:19
  444.2 16.7 %collective-permute-start.10 = (bf16[128,512]{1,0:T(8,128)(2,1)S(1)}, bf16[128,512]{1,0:T(8,128)(2,1)S(1)}, u32[]{:S(2)}, u32[]{:S(2)}) collective-permute-start(bf16[128,512]{1,0:T(8,128)(2,1)S(1)} %collective-permute-done.9), channel_id=1, source_target_pairs={{0,128},{128,0},{8,136},{136,8},{16,144},{144,16},{24,152},{152,24... | collective-permute-start | bytes 393224 | tf_op jit(solution)/shard_map/ppermute | solution.py:19
Sparse Core Ops, SparseCore 0:
  32.0 43.7 all-gather.7
  78.6 84.0 all-gather.15
  165.5 74.6 all-gather.13
  242.8 74.5 all-gather.9
  320.1 74.6 all-gather.11
  474.2 43.1 reduce-scatter.1
where the time goes:
time: 532 us; the launch traced here: 524 us
  waiting for transfers between devices  373 us (70%)
  starting transfers between devices  52.6 us (10%)
  blocking collectives  26.8 us (5%)
  other arithmetic  26.1 us (5%)
  local copies, waits for them, and re-layouts  24.6 us (5%)
  between operations  13.7 us (3%)
  matrix products  5.68 us (1%)
    all_gather x4, waiting for transfers between devices, carried_in(): gathered = jax.tree.map(lambda a: lax.all_gather(a, axis), part)  266 us
    ppermute x10, starting transfers between devices, from_partner(): return lax.ppermute(block, axis, route)  44.3 us
    reduce_scatter x1, waiting for transfers between devices, body(): lax.psum_scatter(summed.astype(jnp.bfloat16), 'ch', scatter_dimension=1,...  43.3 us
    all_gather x1, waiting for transfers between devices, body(): gathered = lax.all_gather(to_gather, 'ch', axis=2, tiled=True)  36.2 us
    psum x1, blocking collectives, body(): inputs_bc = lax.psum(partial_bc, 'ch')  26.8 us
    ppermute x10, waiting for transfers between devices, from_partner(): return lax.ppermute(block, axis, route)  26.2 us
  transfers between devices with their start and end apart: 17, of which 17 were waited for; matrix products, arithmetic and copies ran while one was open for 5% of the time, Pallas kernels for 0%

commit v1 on v0

v1 whole, which is shorter than its diff:
```python
import functools

import jax
import jax.numpy as jnp
from jax import lax
from jax.experimental import pallas as pl
from jax.experimental.pallas import tpu as pltpu
from jax.sharding import PartitionSpec as P

MESH = pl.DeviceIdType.MESH
F32 = jnp.float32
BF16 = jnp.bfloat16
CONV = 4
EPSILON = 1e-05
HALO = 8
SUB = 8
LANES = 128
PER_TURN = 16


def exchange(width, dtype):
    row = lax.broadcasted_iota(jnp.int32, (width, width), 0)
    col = lax.broadcasted_iota(jnp.int32, (width, width), 1)
    return (row + col == width - 1).astype(F32).astype(dtype)


def one_minus_exp(x):
    series = jnp.ones_like(x)
    for order in range(11, 1, -1):
        series = 1.0 - series * x * (1.0 / order)
    return jnp.where(x < 0.5, series * x, 1.0 - jnp.exp(-x))


def silu(x):
    return x * jax.nn.sigmoid(x)


def layer_kernel(
    S, C, L, N,
    tokens_h, bounds, hidden_h, gain_h, embed_h, w_in_h, conv_w_h, conv_b_h, proj_h, rate_h, skip_h, w_out_h,
    out_ref,
    tokens, gain, embed, w_in, conv_w, conv_b, proj, rate, skip, w_cat,
    rows_in, prev_in, next_in, normed,
    x_fore, x_back, z_gate, c_tiles, y_tiles,
    bc_send, bc_recv, b_tiles, r_tiles, a_tiles, g_tiles, block_keep,
    end_send, end_recv, start_send, start_recv,
    y_both, out_send, out_recv,
    local_sem, gather_s, gather_r, prev_s, prev_r, next_s, next_r,
    bc_s, bc_r, end_s, end_r, start_s, start_r, out_s, out_r,
):
    seq = lax.axis_index("seq")
    ch = lax.axis_index("ch")
    halves = 2
    Q = S // halves
    per_owner = N // Q
    half = seq // Q
    own_slot = lax.rem(seq, Q)
    width = hidden_h.shape[1]
    inner = w_in.shape[2]
    chunks = inner // LANES

    def at_seq(offset):
        return lax.rem(seq + offset + S, S)

    def at_ch(offset):
        return lax.rem(ch + offset + C, C)

    fetched = [
        (tokens_h, tokens), (gain_h, gain), (embed_h, embed), (conv_w_h, conv_w), (conv_b_h, conv_b),
        (proj_h, proj), (rate_h, rate), (skip_h, skip), (hidden_h, rows_in.at[ch]),
        (w_in_h.at[0], w_in.at[0]), (w_in_h.at[1], w_in.at[1]),
    ]
    fetched += [
        (w_out_h.at[:, pl.ds(k * width, width)], w_cat.at[k, pl.ds(0, inner)]) for k in range(C)
    ]
    local = [
        pltpu.make_async_copy(src, dst, local_sem.at[k]) for k, (src, dst) in enumerate(fetched)
    ]
    for copy in local:
        copy.start()

    barrier = pltpu.get_barrier_semaphore()
    partners = [(seq, at_ch(d)) for d in range(1, C)]
    partners += [(at_seq(side), at_ch(d)) for side in (1, -1) for d in range(C)]
    partners += [(at_seq(d), ch) for d in range(2, S - 1)]
    for partner in partners:
        pl.semaphore_signal(barrier, inc=1, device_id=partner, device_id_type=MESH)
    pl.semaphore_wait(barrier, len(partners))

    def send(src, dst, send_sem, recv_sem, where):
        copy = pltpu.make_async_remote_copy(
            src_ref=src, dst_ref=dst, send_sem=send_sem, recv_sem=recv_sem,
            device_id=where, device_id_type=MESH,
        )
        copy.start()
        return copy

    gathers = [
        send(hidden_h, rows_in.at[ch], gather_s.at[d], gather_r.at[d], (seq, at_ch(d)))
        for d in range(1, C)
    ]
    halos = []
    for d in range(C):
        halos.append(
            send(
                hidden_h.at[pl.ds(L - HALO, HALO)], prev_in.at[ch], prev_s.at[d], prev_r.at[d],
                (at_seq(1), at_ch(d)),
            )
        )
        halos.append(
            send(
                hidden_h.at[pl.ds(0, HALO)], next_in.at[ch], next_s.at[d], next_r.at[d],
                (at_seq(-1), at_ch(d)),
            )
        )

    for copy in local:
        copy.wait()

    flip = exchange(width, BF16)
    flip_lanes = exchange(LANES, BF16)
    for k in range(C):
        w_cat[k, pl.ds(inner, inner)] = jnp.dot(
            w_cat[C - 1 - k, pl.ds(0, inner)], flip, preferred_element_type=F32
        ).astype(BF16)
    decay = jnp.exp(-rate[...])
    drive = jnp.sqrt(one_minus_exp(2.0 * rate[...]))
    for k in range(SUB):
        part = slice((k % chunks) * LANES, (k % chunks + 1) * LANES)
        a_tiles[pl.ds(k, N, stride=SUB), :] = decay[:, part]
        g_tiles[pl.ds(k, N, stride=SUB), :] = drive[:, part]

    def keep_at(places):
        hits = jnp.zeros(places.shape, F32)
        for i in range(bounds.shape[0]):
            for j in range(bounds.shape[1]):
                hits = hits + (places == bounds[i, j]).astype(F32)
        return 1.0 / (1.0 + hits)

    lane = lax.broadcasted_iota(jnp.int32, (S, LANES), 1)
    kept = keep_at(lax.broadcasted_iota(jnp.int32, (S, LANES), 0) * L + lane)
    shift = LANES // 2
    while shift:
        kept = kept * pltpu.roll(kept, shift, 1)
        shift //= 2
    block_keep[...] = kept

    lane_row = lax.broadcasted_iota(jnp.int32, (SUB, LANES), 1)

    def running_keep(places):
        run = keep_at(places)
        step = 1
        while step < LANES:
            run = run * jnp.where(lane_row >= step, pltpu.roll(run, step, 1), 1.0)
            step *= 2
        return run[0:1]

    keep_fore = running_keep(seq * L + lane_row)
    keep_back = running_keep(seq * L + (L - 1) - lane_row)

    def base_of(block):
        row = tokens[pl.ds(block, 1), :].astype(F32)
        return jnp.broadcast_to(row, (LANES, LANES)).T[:, 0:1]

    own_base = base_of(seq)
    prev_base = base_of(at_seq(-1))[L - HALO :]
    next_base = base_of(at_seq(1))[:HALO]

    for copy in gathers:
        copy.wait_recv()
    for copy in halos:
        copy.wait_recv()

    def norm_into(block, base, emit):
        total = jnp.zeros((block.shape[1], 1), F32)
        for k in range(C):
            part = block[k].astype(F32)
            total = total + jnp.sum(part * part, axis=1, keepdims=True)
        inv_rms = lax.rsqrt(total * (1.0 / (C * width)) + EPSILON)
        for k in range(C):
            cols = slice(k * width, (k + 1) * width)
            added = jnp.where(base == 0.0, embed[0:1, cols], embed[1:2, cols])
            added = jnp.where(base == 2.0, embed[2:3, cols], added)
            added = jnp.where(base == 3.0, embed[3:4, cols], added)
            emit(k, (block[k].astype(F32) * inv_rms * gain[0:1, cols] + added).astype(BF16))

    def flipped(part):
        return jnp.dot(part, flip, preferred_element_type=F32).astype(BF16)

    def emit_own(k, part):
        normed[0:L, k * width : (k + 1) * width] = part
        k = C - 1 - k
        normed[L : 2 * L, k * width : (k + 1) * width] = flipped(part)

    edge_prev = []
    edge_next = []
    norm_into(rows_in, own_base, emit_own)
    norm_into(prev_in, prev_base, lambda k, part: edge_prev.append(part))
    norm_into(next_in, next_base, lambda k, part: edge_next.append(part))
    for k in range(C):
        both = jnp.concatenate([edge_prev[k], edge_next[k]], axis=0)
        turned = flipped(jnp.concatenate([edge_prev[C - 1 - k], edge_next[C - 1 - k]], axis=0))
        top = lax.broadcasted_iota(jnp.int32, both.shape, 0) < HALO
        normed[2 * L :, k * width : (k + 1) * width] = jnp.where(top, both, turned)

    x_all = jnp.dot(normed[...], w_in[0], preferred_element_type=F32).astype(BF16).astype(F32)
    has_prev = jnp.where(seq > 0, 1.0, 0.0)
    has_next = jnp.where(seq < S - 1, 1.0, 0.0)
    x_fore[0:HALO] = x_all[2 * L : 2 * L + HALO] * has_prev
    x_fore[HALO:] = x_all[0:L]
    x_back[0:L] = x_all[L : 2 * L]
    x_back[L:] = x_all[2 * L + HALO :] * has_next
    sum_fore = jnp.broadcast_to(conv_b[...], (L, inner))
    sum_back = sum_fore
    for k in range(CONV):
        tap = conv_w[k : k + 1, :]
        sum_fore = sum_fore + x_fore[pl.ds(HALO - CONV + 1 + k, L), :] * tap
        sum_back = sum_back + x_back[pl.ds(CONV - 1 - k, L), :] * tap
    c_fore = silu(sum_fore).astype(BF16)
    c_back = silu(sum_back).astype(BF16)

    nt = (((1,), (1,)), ((), ()))
    part_fore = lax.dot_general(proj[...], c_fore, nt, preferred_element_type=F32).astype(BF16)
    part_back = lax.dot_general(proj[...], c_back, nt, preferred_element_type=F32).astype(BF16)
    bc_send[0 : 2 * N] = part_fore
    bc_send[2 * N :] = jnp.dot(part_back, flip_lanes, preferred_element_type=F32).astype(BF16)
    shares = [
        send(bc_send, bc_recv.at[d], bc_s.at[d], bc_r.at[d], (seq, at_ch(d))) for d in range(1, C)
    ]
    for k in range(chunks):
        part = slice(k * LANES, (k + 1) * LANES)
        c_tiles[pl.ds(k, L, stride=SUB), :] = c_fore[:, part].astype(F32)
        c_tiles[pl.ds(chunks + k, L, stride=SUB), :] = c_back[:, part].astype(F32)
    z_all = jnp.dot(normed[0 : 2 * L], w_in[1], preferred_element_type=F32).astype(BF16)
    z_gate[...] = silu(z_all.astype(F32))
    for copy in shares:
        copy.wait_recv()
    bc = bc_send[...].astype(F32)
    for d in range(1, C):
        bc = bc + bc_recv[d].astype(F32)
    b_fore = bc[0:N] / keep_fore
    r_fore = bc[N : 2 * N] * keep_fore
    b_back = bc[2 * N : 3 * N] / keep_back
    r_back = bc[3 * N :] * keep_back
    for k in range(SUB):
        b_tiles[pl.ds(k, N, stride=SUB), :] = b_fore if k < chunks else b_back
        r_tiles[pl.ds(k, N, stride=SUB), :] = r_fore if k < chunks else r_back

    upper = lax.broadcasted_iota(jnp.int32, (SUB, LANES), 0) < chunks

    def tile(ref, n):
        return ref[pl.ds(n * SUB, SUB), :]

    def across(ref, n, s):
        return jnp.broadcast_to(tile(ref, n)[:, s : s + 1], (SUB, LANES))

    def turn_lanes(ref):
        for n in range(N):
            ref[pl.ds(n * SUB, SUB), :] = pltpu.roll(tile(ref, n), LANES - PER_TURN, 1)

    def step_rows(j):
        fore = pl.multiple_of(j * SUB, SUB)
        back = pl.multiple_of((L - 1 - j) * SUB, SUB)
        return fore, back

    def local_turn(i, states):
        states = list(states)
        for s in range(PER_TURN):
            fore, back = step_rows(i * PER_TURN + s)
            x = jnp.where(upper, c_tiles[pl.ds(fore, SUB), :], c_tiles[pl.ds(back, SUB), :])
            y = jnp.zeros((SUB, LANES), F32)
            for n in range(N):
                states[n] = tile(a_tiles, n) * states[n] + across(b_tiles, n, s) * x
                y = y + across(r_tiles, n, s) * (tile(g_tiles, n) * states[n])
            y_tiles[pl.ds(fore, chunks), :] = y[0:chunks]
            y_tiles[pl.ds(back + chunks, chunks), :] = y[chunks:]
        turn_lanes(b_tiles)
        turn_lanes(r_tiles)
        return tuple(states)

    zeros = tuple(jnp.zeros((SUB, LANES), F32) for _ in range(N))
    states = lax.fori_loop(0, L // PER_TURN, local_turn, zeros)

    own_keep = block_keep[pl.ds(seq, 1), :]
    for n in range(N):
        end_send[n] = own_keep * states[n]
    ends = []
    for d in range(1, S):
        to = at_seq(d)
        mine = pl.ds(lax.rem(to, Q) * per_owner, per_owner)
        ends.append(
            send(end_send.at[mine], end_recv.at[seq], end_s.at[d], end_r.at[d], (to, ch))
        )
    own_n = pl.ds(own_slot * per_owner, per_owner)
    end_recv[seq] = end_send[own_n]
    for copy in ends:
        copy.wait_recv()
    tile_rows = pl.ds(pl.multiple_of(own_slot * per_owner * SUB, SUB), per_owner * SUB)
    block_decay = a_tiles[tile_rows, :]
    for _ in range(L.bit_length() - 1):
        block_decay = block_decay * block_decay
    block_decay = block_decay.reshape(per_owner, SUB, LANES)
    value = jnp.zeros((per_owner, SUB, LANES), F32)
    for s in range(S):
        far = S - 1 - s
        start_send[s, :, 0:chunks] = value[:, 0:chunks]
        start_send[far, :, chunks:] = value[:, chunks:]
        ended = jnp.where(upper, end_recv[s], end_recv[far])
        kept = jnp.where(upper, block_keep[s : s + 1, :], block_keep[far : far + 1, :])
        value = ended + kept * block_decay * value
    starts = []
    for d in range(1, Q):
        to = half * Q + lax.rem(own_slot + d, Q)
        starts.append(
            send(start_send.at[to], start_recv.at[own_slot], start_s.at[d], start_r.at[d], (to, ch))
        )
    start_recv[own_slot] = start_send[seq]
    for copy in starts:
        copy.wait_recv()

    entering = []
    for n in range(N):
        entering.append(tile(g_tiles, n) * start_recv[n // per_owner, n % per_owner])

    def entering_turn(i, states):
        states = list(states)
        for s in range(PER_TURN):
            fore, back = step_rows(i * PER_TURN + s)
            y = jnp.zeros((SUB, LANES), F32)
            for n in range(N):
                states[n] = tile(a_tiles, n) * states[n]
                y = y + across(r_tiles, n, s) * states[n]
            here = pl.ds(fore, chunks)
            there = pl.ds(back + chunks, chunks)
            y_tiles[here, :] = y_tiles[here, :] + y[0:chunks]
            y_tiles[there, :] = y_tiles[there, :] + y[chunks:]
        turn_lanes(r_tiles)
        return tuple(states)

    lax.fori_loop(0, L // PER_TURN, entering_turn, tuple(entering))

    for k in range(2 * chunks):
        part = slice((k % chunks) * LANES, (k % chunks + 1) * LANES)
        at = pl.ds(k, L, stride=SUB)
        row = (k // chunks) * L
        y = y_tiles[at, :] + skip[0:1, part] * c_tiles[at, :]
        y_both[:, k * LANES : (k + 1) * LANES] = (y * z_gate[row : row + L, part]).astype(BF16)

    sums = []
    for d in range(1, C):
        out_send[d] = jnp.dot(y_both[...], w_cat[at_ch(d)], preferred_element_type=F32).astype(BF16)
        sums.append(
            send(out_send.at[d], out_recv.at[d], out_s.at[d], out_r.at[d], (seq, at_ch(d)))
        )
    total = jnp.dot(y_both[...], w_cat[ch], preferred_element_type=F32)
    for d, copy in enumerate(sums):
        copy.wait_recv()
        total = total + out_recv[d + 1].astype(F32)
    out_ref[...] = total.astype(BF16)

    for copy in gathers + halos + shares + ends + starts + sums:
        copy.wait_send()


def solution(mesh):
    S, C = mesh.shape["seq"], mesh.shape["ch"]

    def body(
        hidden, tokens, edit_bounds, norm_gain, base_embed, w_in, conv_w, conv_b, proj_bc, decay_rate, skip_gain, w_out
    ):
        L, width = hidden.shape
        N, inner = decay_rate.shape
        D = C * width
        Q = S // 2
        per_owner = N // Q
        any_space = pl.BlockSpec(memory_space=pl.ANY)
        vmem = pltpu.VMEM
        dma = pltpu.SemaphoreType.DMA
        return pl.pallas_call(
            functools.partial(layer_kernel, S, C, L, N),
            out_shape=jax.ShapeDtypeStruct((L, width), BF16),
            in_specs=[any_space, pl.BlockSpec(memory_space=pltpu.SMEM)] + [any_space] * 10,
            out_specs=pl.BlockSpec(memory_space=pltpu.VMEM),
            scratch_shapes=[
                vmem((S, L), jnp.int32), vmem((1, D), F32), vmem((4, D), F32),
                vmem((2, D, inner), BF16), vmem((CONV, inner), F32), vmem((1, inner), F32),
                vmem((2 * N, inner), BF16), vmem((N, inner), F32), vmem((1, inner), F32),
                vmem((C, 2 * inner, width), BF16),
                vmem((C, L, width), BF16), vmem((C, HALO, width), BF16), vmem((C, HALO, width), BF16),
                vmem((2 * L + 2 * HALO, D), BF16),
                vmem((L + HALO, inner), F32), vmem((L + HALO, inner), F32), vmem((2 * L, inner), F32),
                vmem((L * SUB, LANES), F32), vmem((L * SUB, LANES), F32),
                vmem((4 * N, LANES), BF16), vmem((C, 4 * N, LANES), BF16),
                vmem((N * SUB, LANES), F32), vmem((N * SUB, LANES), F32),
                vmem((N * SUB, LANES), F32), vmem((N * SUB, LANES), F32), vmem((S, LANES), F32),
                vmem((N, SUB, LANES), F32), vmem((S, per_owner, SUB, LANES), F32),
                vmem((S, per_owner, SUB, LANES), F32), vmem((Q, per_owner, SUB, LANES), F32),
                vmem((L, 2 * inner), BF16), vmem((C, L, width), BF16), vmem((C, L, width), BF16),
                dma((11 + C,)), dma((C,)), dma((C,)), dma((C,)), dma((C,)), dma((C,)), dma((C,)),
                dma((C,)), dma((C,)), dma((S,)), dma((S,)), dma((Q,)), dma((Q,)), dma((C,)), dma((C,)),
            ],
            compiler_params=pltpu.CompilerParams(
                collective_id=0, has_side_effects=True, vmem_limit_bytes=60 * 1024 * 1024
            ),
            name="layer",
        )(
            tokens.reshape(S, L), edit_bounds.T, hidden, norm_gain.reshape(1, D), base_embed, w_in,
            conv_w, conv_b.reshape(1, inner), proj_bc, decay_rate, skip_gain.reshape(1, inner), w_out,
        )

    placed = (
        P("seq", "ch"), P(), P(), P(), P(), P(None, None, "ch"), P(None, "ch"), P("ch"),
        P(None, "ch"), P(None, "ch"), P("ch"), P("ch", None),
    )
    return jax.shard_map(
        body, mesh=mesh, in_specs=placed, out_specs=P("seq", "ch"), check_vma=False
    )
```

time: 532 us -> 62.3 us (0.12); the launches traced: 524 us -> 62.2 us
  waiting for transfers between devices: 373 us -> 0 us
  Pallas kernels: 0 us -> 60.7 us
  starting transfers between devices: 52.6 us -> 0 us
  blocking collectives: 26.8 us -> 0 us
  other arithmetic: 26.1 us -> 0 us
  local copies, waits for them, and re-layouts: 24.6 us -> 1.47 us
  between operations: 13.7 us -> 0.01 us
  matrix products: 5.68 us -> 0 us
    all_gather x5 -> x0, waiting for transfers between devices: 302 us -> none  [the longest x4 266 us: carried_in(): gathered = jax.tree.map(lambda a: lax.all_gather(a, axis), part)]
    pallas_call x0 -> x1, Pallas kernels: none -> 60.7 us  [body(): pl.pallas_call(functools.partial(layer_kernel, S, C, L, N), out_shape=jax...]
    ppermute x11 -> x0, starting transfers between devices: 52.4 us -> none  [the longest x10 44.3 us: from_partner(): return lax.ppermute(block, axis, route)]
    reduce_scatter x1 -> x0, waiting for transfers between devices: 43.3 us -> none  [body(): lax.psum_scatter(summed.astype(jnp.bfloat16), 'ch', scatter_dimension=1,...]
    psum x1 -> x0, blocking collectives: 26.8 us -> none  [body(): inputs_bc = lax.psum(partial_bc, 'ch')]
    ppermute x11 -> x0, waiting for transfers between devices: 26.8 us -> none  [the longest x10 26.2 us: from_partner(): return lax.ppermute(block, axis, route)]
    rev x3 -> x0, local copies, waits for them, and re-layouts: 11.3 us -> none  [the longest x1 9.34 us: body(): jnp.dot(aligned, w_out, preferred_element_type=jnp.float32)[:, ::-1]]
    reduce_sum x42 -> x0, other arithmetic: 9.6 us -> none  [the longest x40 8.03 us: turn_step(): outputs.append(jnp.sum(r_block[row_index][:, :, None] * state, axis=1))]
  transfers between devices with their start and end apart: 17 -> 0, of which waited for: 17 -> 0; matrix products, arithmetic and copies ran while one was open for 5% -> 0% of each run, Pallas kernels for 0% -> 0%
where the time goes in v1:
time: 62.3 us; the launch traced here: 62.2 us
  Pallas kernels  60.7 us (97%)
  local copies, waits for them, and re-layouts  1.47 us (2%)
    pallas_call x1, Pallas kernels, body(): pl.pallas_call(functools.partial(layer_kernel, S, C, L, N), out_shape=jax...  60.7 us
    unnamed x1, local copies, waits for them, and re-layouts  1.47 us

profile of v1, /device:TPU:1, one launch (start us, length us, event | category | flops | bytes accessed | tf_op | source)
XLA Modules:
  0.0 62.2 jit_solution(2228189194781193994)
XLA Ops:
  0.0 60.7 %layer.1 = bf16[128,256]{1,0:T(8,128)(2,1)} custom-call(s32[32,128]{1,0:T(8,128)} %bitcast.5, s32[2,8]{1,0:T(2,128)} %bitcast.9, bf16[128,256]{1,0:T(8,128)(2,1)} %hidden_h.1, f32[1,2048]{1,0:T(1,128)} %bitcast.6, f32[4,2048]{1,0:T(4,128)} %embed_h.1, bf16[2,2048,512]{2,1,0:T(8,128)(2,1)} %w_in_h.1, f32[4,512]{1,0:T(4,128)} %conv_w_h.1, f32[1,512]{1,0:T(1,128)} %bitcast.7, ...), custom_call_target="tpu_custom_call" | custom-call | tf_op jit(solution)/shard_map/layer/pallas_call | solution.py:379
  60.7 1.5 %copy.14 = bf16[128,256]{1,0:T(8,128)(2,1)} copy(bf16[128,256]{1,0:T(8,128)(2,1)} %layer.1) | data formatting | bytes 131072

commit v2 on v1

--- a/solution.py
+++ b/solution.py
@@ -11,11 +11,13 @@
 F32 = jnp.float32
 BF16 = jnp.bfloat16
 CONV = 4
+REGION = 4
 EPSILON = 1e-05
 HALO = 8
 SUB = 8
 LANES = 128
 PER_TURN = 16
+EARLY_TURNS = 6
 
 
 def exchange(width, dtype):
@@ -41,20 +43,17 @@
     out_ref,
     tokens, gain, embed, w_in, conv_w, conv_b, proj, rate, skip, w_cat,
     rows_in, prev_in, next_in, normed,
-    x_fore, x_back, z_gate, c_tiles, y_tiles,
-    bc_send, bc_recv, b_tiles, r_tiles, a_tiles, g_tiles, block_keep,
-    end_send, end_recv, start_send, start_recv,
+    x_fore, x_back, z_gate, c_rows, c_tiles, y_tiles,
+    bc_send, bc_recv, b_lanes, b_tiles, r_tiles, decay_rows, a_tiles, g_tiles, block_keep, block_decay,
+    end_send, end_recv, start_send, start_recv, v_tiles, t_tiles,
     y_both, out_send, out_recv,
     local_sem, gather_s, gather_r, prev_s, prev_r, next_s, next_r,
-    bc_s, bc_r, end_s, end_r, start_s, start_r, out_s, out_r,
+    bc_s, bc_r, end_s, end_r, near_s, near_r, start_s, start_r, out_s, out_r,
 ):
     seq = lax.axis_index("seq")
     ch = lax.axis_index("ch")
-    halves = 2
-    Q = S // halves
-    per_owner = N // Q
-    half = seq // Q
-    own_slot = lax.rem(seq, Q)
+    region = seq // REGION
+    member = lax.rem(seq, REGION)
     width = hidden_h.shape[1]
     inner = w_in.shape[2]
     chunks = inner // LANES
@@ -125,6 +124,12 @@
         ).astype(BF16)
     decay = jnp.exp(-rate[...])
     drive = jnp.sqrt(one_minus_exp(2.0 * rate[...]))
+    decay_rows[...] = decay
+    long_decay = decay
+    for _ in range(L.bit_length() - 1):
+        long_decay = long_decay * long_decay
+    for k in range(chunks):
+        block_decay[k] = long_decay[:, k * LANES : (k + 1) * LANES]
     for k in range(SUB):
         part = slice((k % chunks) * LANES, (k % chunks + 1) * LANES)
         a_tiles[pl.ds(k, N, stride=SUB), :] = decay[:, part]
@@ -229,6 +234,8 @@
     ]
     for k in range(chunks):
         part = slice(k * LANES, (k + 1) * LANES)
+        c_rows[k] = c_fore[:, part].astype(F32)
+        c_rows[chunks + k] = c_back[:, part].astype(F32)
         c_tiles[pl.ds(k, L, stride=SUB), :] = c_fore[:, part].astype(F32)
         c_tiles[pl.ds(chunks + k, L, stride=SUB), :] = c_back[:, part].astype(F32)
     z_all = jnp.dot(normed[0 : 2 * L], w_in[1], preferred_element_type=F32).astype(BF16)
@@ -242,10 +249,63 @@
     r_fore = bc[N : 2 * N] * keep_fore
     b_back = bc[2 * N : 3 * N] / keep_back
     r_back = bc[3 * N :] * keep_back
+    b_lanes[0] = b_fore
+    b_lanes[1] = b_back
     for k in range(SUB):
         b_tiles[pl.ds(k, N, stride=SUB), :] = b_fore if k < chunks else b_back
         r_tiles[pl.ds(k, N, stride=SUB), :] = r_fore if k < chunks else r_back
 
+    def end_turn(i, states):
+        states = list(states)
+        for s in range(PER_TURN):
+            at = i * PER_TURN + s
+            for way in range(2):
+                row = at if way == 0 else L - 1 - at
+                b = b_lanes[way]
+                b = [
+                    jnp.broadcast_to(b[h * SUB : (h + 1) * SUB, s : s + 1], (SUB, LANES))
+                    for h in range(N // SUB)
+                ]
+                for k in range(chunks):
+                    part = pl.ds(k * LANES, LANES)
+                    x = c_rows[way * chunks + k, pl.ds(row, SUB, stride=0), :]
+                    for h in range(N // SUB):
+                        slot = (way * chunks + k) * (N // SUB) + h
+                        states[slot] = decay_rows[pl.ds(h * SUB, SUB), part] * states[slot] + b[h] * x
+        for way in range(2):
+            b_lanes[way] = pltpu.roll(b_lanes[way], LANES - PER_TURN, 1)
+        return tuple(states)
+
+    zeros = tuple(jnp.zeros((SUB, LANES), F32) for _ in range(N))
+    ended = lax.fori_loop(0, L // PER_TURN, end_turn, zeros)
+    own_keep = block_keep[pl.ds(seq, 1), :]
+    for way in range(2):
+        for k in range(chunks):
+            slot = (way * chunks + k) * (N // SUB)
+            whole = jnp.concatenate(ended[slot : slot + N // SUB], axis=0)
+            end_send[way, k] = (own_keep * whole).astype(BF16)
+
+    ends = []
+    for d in range(1, S):
+        to = at_seq(d)
+        way = jnp.where(to // REGION < region, 1, 0)
+        ends.append(
+            send(
+                end_send.at[way, lax.rem(to, REGION)], end_recv.at[way, seq], end_s.at[d], end_r.at[d],
+                (to, ch),
+            )
+        )
+    for d in range(1, REGION):
+        to_member = lax.rem(member + d, REGION)
+        ends.append(
+            send(
+                end_send.at[1, to_member], end_recv.at[1, seq], near_s.at[d], near_r.at[d],
+                (region * REGION + to_member, ch),
+            )
+        )
+    for way in range(2):
+        end_recv[way, seq] = end_send[way, member]
+
     upper = lax.broadcasted_iota(jnp.int32, (SUB, LANES), 0) < chunks
 
     def tile(ref, n):
@@ -258,93 +318,99 @@
         for n in range(N):
             ref[pl.ds(n * SUB, SUB), :] = pltpu.roll(tile(ref, n), LANES - PER_TURN, 1)
 
-    def step_rows(j):
-        fore = pl.multiple_of(j * SUB, SUB)
-        back = pl.multiple_of((L - 1 - j) * SUB, SUB)
-        return fore, back
+    def tile_rows(j):
+        return pl.ds(pl.multiple_of(j * SUB, SUB), SUB)
+
+    for n in range(N):
+        v_tiles[pl.ds(n * SUB, SUB), :] = tile(a_tiles, n) * tile(g_tiles, n)
 
     def local_turn(i, states):
         states = list(states)
         for s in range(PER_TURN):
-            fore, back = step_rows(i * PER_TURN + s)
-            x = jnp.where(upper, c_tiles[pl.ds(fore, SUB), :], c_tiles[pl.ds(back, SUB), :])
-            y = jnp.zeros((SUB, LANES), F32)
+            j = i * PER_TURN + s
+            x = jnp.where(upper, c_tiles[tile_rows(j), :], c_tiles[tile_rows(L - 1 - j), :])
+            y = skip_tile * x
             for n in range(N):
                 states[n] = tile(a_tiles, n) * states[n] + across(b_tiles, n, s) * x
-                y = y + across(r_tiles, n, s) * (tile(g_tiles, n) * states[n])
-            y_tiles[pl.ds(fore, chunks), :] = y[0:chunks]
-            y_tiles[pl.ds(back + chunks, chunks), :] = y[chunks:]
+                r = across(r_tiles, n, s)
+                y = y + r * (tile(g_tiles, n) * states[n])
+                reach = tile(v_tiles, n)
+                t_tiles[j * N + n] = r * reach
+                v_tiles[pl.ds(n * SUB, SUB), :] = reach * tile(a_tiles, n)
+            y_tiles[tile_rows(j), :] = y
         turn_lanes(b_tiles)
         turn_lanes(r_tiles)
         return tuple(states)
 
-    zeros = tuple(jnp.zeros((SUB, LANES), F32) for _ in range(N))
-    states = lax.fori_loop(0, L // PER_TURN, local_turn, zeros)
-
-    own_keep = block_keep[pl.ds(seq, 1), :]
-    for n in range(N):
-        end_send[n] = own_keep * states[n]
-    ends = []
-    for d in range(1, S):
-        to = at_seq(d)
-        mine = pl.ds(lax.rem(to, Q) * per_owner, per_owner)
-        ends.append(
-            send(end_send.at[mine], end_recv.at[seq], end_s.at[d], end_r.at[d], (to, ch))
-        )
-    own_n = pl.ds(own_slot * per_owner, per_owner)
-    end_recv[seq] = end_send[own_n]
+    skip_tile = jnp.concatenate(
+        [skip[0:1, (k % chunks) * LANES : (k % chunks + 1) * LANES] for k in range(SUB)], axis=0
+    )
+    turns = L // PER_TURN
+    states = lax.fori_loop(0, EARLY_TURNS, local_turn, zeros)
+
     for copy in ends:
         copy.wait_recv()
-    tile_rows = pl.ds(pl.multiple_of(own_slot * per_owner * SUB, SUB), per_owner * SUB)
-    block_decay = a_tiles[tile_rows, :]
-    for _ in range(L.bit_length() - 1):
-        block_decay = block_decay * block_decay
-    block_decay = block_decay.reshape(per_owner, SUB, LANES)
-    value = jnp.zeros((per_owner, SUB, LANES), F32)
-    for s in range(S):
-        far = S - 1 - s
-        start_send[s, :, 0:chunks] = value[:, 0:chunks]
-        start_send[far, :, chunks:] = value[:, chunks:]
-        ended = jnp.where(upper, end_recv[s], end_recv[far])
-        kept = jnp.where(upper, block_keep[s : s + 1, :], block_keep[far : far + 1, :])
-        value = ended + kept * block_decay * value
+    decay_here = block_decay[member]
+
+    def carry_on(way, i, value):
+        factor = block_keep[pl.ds(i, 1), :] * decay_here
+        return end_recv[way, i].astype(F32) + factor * value
+
+    def fore_region(g, value):
+        for k in range(REGION):
+            value = carry_on(0, g * REGION + k, value)
+        return value
+
+    def back_region(g, value):
+        for k in range(REGION):
+            value = carry_on(1, S - 1 - (g * REGION + k), value)
+        return value
+
+    value = lax.fori_loop(0, region, fore_region, jnp.zeros((N, LANES), F32))
+    for k in range(REGION):
+        start_send[k, 0] = value.astype(BF16)
+        value = carry_on(0, region * REGION + k, value)
+    value = lax.fori_loop(0, S // REGION - 1 - region, back_region, jnp.zeros((N, LANES), F32))
+    for k in range(REGION - 1, -1, -1):
+        start_send[k, 1] = value.astype(BF16)
+        value = carry_on(1, region * REGION + k, value)
     starts = []
-    for d in range(1, Q):
-        to = half * Q + lax.rem(own_slot + d, Q)
+    for d in range(1, REGION):
+        to_member = lax.rem(member + d, REGION)
         starts.append(
-            send(start_send.at[to], start_recv.at[own_slot], start_s.at[d], start_r.at[d], (to, ch))
-        )
-    start_recv[own_slot] = start_send[seq]
+            send(
+                start_send.at[to_member], start_recv.at[member], start_s.at[d], start_r.at[d],
+                (region * REGION + to_member, ch),
+            )
+        )
+    start_recv[member] = start_send[member]
+    lax.fori_loop(EARLY_TURNS, turns, local_turn, states)
     for copy in starts:
         copy.wait_recv()
 
-    entering = []
-    for n in range(N):
-        entering.append(tile(g_tiles, n) * start_recv[n // per_owner, n % per_owner])
-
-    def entering_turn(i, states):
-        states = list(states)
-        for s in range(PER_TURN):
-            fore, back = step_rows(i * PER_TURN + s)
-            y = jnp.zeros((SUB, LANES), F32)
-            for n in range(N):
-                states[n] = tile(a_tiles, n) * states[n]
-                y = y + across(r_tiles, n, s) * states[n]
-            here = pl.ds(fore, chunks)
-            there = pl.ds(back + chunks, chunks)
-            y_tiles[here, :] = y_tiles[here, :] + y[0:chunks]
-            y_tiles[there, :] = y_tiles[there, :] + y[chunks:]
-        turn_lanes(r_tiles)
-        return tuple(states)
-
-    lax.fori_loop(0, L // PER_TURN, entering_turn, tuple(entering))
+    for k in range(SUB):
+        v_tiles[pl.ds(k, N, stride=SUB), :] = start_recv[k % chunks, k // chunks].astype(F32)
+    entering = [tile(v_tiles, n) for n in range(N)]
+
+    def entering_turn(i, carried):
+        for s in range(SUB):
+            j = i * SUB + s
+            parts = [t_tiles[j * N + n] * entering[n] for n in range(N)]
+            while len(parts) > 1:
+                parts = [parts[k] + parts[k + 1] for k in range(0, len(parts), 2)]
+            y = y_tiles[tile_rows(j), :] + parts[0]
+            c_tiles[pl.ds(pl.multiple_of(j * SUB, SUB), chunks), :] = y[0:chunks]
+            there = pl.multiple_of((L - 1 - j) * SUB, SUB) + chunks
+            c_tiles[pl.ds(there, chunks), :] = y[chunks:]
+        return carried
+
+    lax.fori_loop(0, L // SUB, entering_turn, 0)
 
     for k in range(2 * chunks):
         part = slice((k % chunks) * LANES, (k % chunks + 1) * LANES)
-        at = pl.ds(k, L, stride=SUB)
         row = (k // chunks) * L
-        y = y_tiles[at, :] + skip[0:1, part] * c_tiles[at, :]
-        y_both[:, k * LANES : (k + 1) * LANES] = (y * z_gate[row : row + L, part]).astype(BF16)
+        y = c_tiles[pl.ds(k, L, stride=SUB), :] * z_gate[row : row + L, part]
+        y_both[:, k * LANES : (k + 1) * LANES] = y.astype(BF16)
 
     sums = []
     for d in range(1, C):
@@ -371,8 +437,7 @@
         L, width = hidden.shape
         N, inner = decay_rate.shape
         D = C * width
-        Q = S // 2
-        per_owner = N // Q
+        chunks = inner // LANES
         any_space = pl.BlockSpec(memory_space=pl.ANY)
         vmem = pltpu.VMEM
         dma = pltpu.SemaphoreType.DMA
@@ -389,15 +454,18 @@
                 vmem((C, L, width), BF16), vmem((C, HALO, width), BF16), vmem((C, HALO, width), BF16),
                 vmem((2 * L + 2 * HALO, D), BF16),
                 vmem((L + HALO, inner), F32), vmem((L + HALO, inner), F32), vmem((2 * L, inner), F32),
-                vmem((L * SUB, LANES), F32), vmem((L * SUB, LANES), F32),
+                vmem((2 * chunks, L, LANES), F32), vmem((L * SUB, LANES), F32), vmem((L * SUB, LANES), F32),
                 vmem((4 * N, LANES), BF16), vmem((C, 4 * N, LANES), BF16),
-                vmem((N * SUB, LANES), F32), vmem((N * SUB, LANES), F32),
-                vmem((N * SUB, LANES), F32), vmem((N * SUB, LANES), F32), vmem((S, LANES), F32),
-                vmem((N, SUB, LANES), F32), vmem((S, per_owner, SUB, LANES), F32),
-                vmem((S, per_owner, SUB, LANES), F32), vmem((Q, per_owner, SUB, LANES), F32),
+                vmem((2, N, LANES), F32), vmem((N * SUB, LANES), F32), vmem((N * SUB, LANES), F32),
+                vmem((N, inner), F32), vmem((N * SUB, LANES), F32), vmem((N * SUB, LANES), F32),
+                vmem((S, LANES), F32), vmem((chunks, N, LANES), F32),
+                vmem((2, chunks, N, LANES), BF16), vmem((2, S, N, LANES), BF16),
+                vmem((REGION, 2, N, LANES), BF16), vmem((REGION, 2, N, LANES), BF16),
+                vmem((N * SUB, LANES), F32), vmem((L * N, SUB, LANES), F32),
                 vmem((L, 2 * inner), BF16), vmem((C, L, width), BF16), vmem((C, L, width), BF16),
                 dma((11 + C,)), dma((C,)), dma((C,)), dma((C,)), dma((C,)), dma((C,)), dma((C,)),
-                dma((C,)), dma((C,)), dma((S,)), dma((S,)), dma((Q,)), dma((Q,)), dma((C,)), dma((C,)),
+                dma((C,)), dma((C,)), dma((S,)), dma((S,)), dma((REGION,)), dma((REGION,)),
+                dma((REGION,)), dma((REGION,)), dma((C,)), dma((C,)),
             ],
             compiler_params=pltpu.CompilerParams(
                 collective_id=0, has_side_effects=True, vmem_limit_bytes=60 * 1024 * 1024

time: 62.3 us -> 51.2 us (0.82)
  Pallas kernels: 60.7 us -> 49.6 us
    pallas_call x1, Pallas kernels: 60.7 us -> 49.6 us  [body(): pl.pallas_call(functools.partial(layer_kernel, S, C, L, N), out_shape=jax...]
where the time goes in v2:
time: 51.2 us; the launch traced here: 51.1 us
  Pallas kernels  49.6 us (97%)
  local copies, waits for them, and re-layouts  1.47 us (3%)
    pallas_call x1, Pallas kernels, body(): pl.pallas_call(functools.partial(layer_kernel, S, C, L, N), out_shape=jax...  49.6 us
    unnamed x1, local copies, waits for them, and re-layouts  1.47 us

profile of v2, /device:TPU:1, one launch (start us, length us, event | category | flops | bytes accessed | tf_op | source)
XLA Modules:
  0.0 51.1 jit_solution(6427910787791670376)
XLA Ops:
  0.0 49.6 %layer.1 = bf16[128,256]{1,0:T(8,128)(2,1)} custom-call(s32[32,128]{1,0:T(8,128)} %bitcast.5, s32[2,8]{1,0:T(2,128)} %bitcast.9, bf16[128,256]{1,0:T(8,128)(2,1)} %hidden_h.1, f32[1,2048]{1,0:T(1,128)} %bitcast.6, f32[4,2048]{1,0:T(4,128)} %embed_h.1, bf16[2,2048,512]{2,1,0:T(8,128)(2,1)} %w_in_h.1, f32[4,512]{1,0:T(4,128)} %conv_w_h.1, f32[1,512]{1,0:T(1,128)} %bitcast.7, ...), custom_call_target="tpu_custom_call" | custom-call | tf_op jit(solution)/shard_map/layer/pallas_call | solution.py:444
  49.6 1.5 %copy.14 = bf16[128,256]{1,0:T(8,128)(2,1)} copy(bf16[128,256]{1,0:T(8,128)(2,1)} %layer.1) | data formatting | bytes 131072
